TPU v7x, 512 devices: a whole 4x8x8 slice. The times are simulated.
512 devices in a mesh: layer: 32 (over z_lo, x, core), dp: 8 (over y), mp: 2 (over z_hi).
Axes of the slice: x: 4, y: 8, z: 8 (z_hi: 2, z_lo: 4; z = z_hi * 4 + z_lo), core: 2. Of those that a mesh axis runs over, the one named last changes fastest.
Arguments:
- states: bfloat16 [128, 1024, 1024], P('layer', 'dp'), may hold values from -6 to 6
- weights: bfloat16 [128, 1024, 1024], P('layer', 'dp', 'mp'), may hold values from -0.1875 to 0.1875
- guess_points: bfloat16 [32, 1024, 1024], P('layer', 'dp'), may hold values from -2 to 2
- cotangent: bfloat16 [1024, 1024], P('dp'), may hold values from -6 to 6
Outputs:
- adjoint: bfloat16 [128, 1024, 1024], P('layer', 'dp', 'mp')
- weight_grads: float32 [128, 1024, 1024], P('layer', 'dp', 'mp')
All inputs are finite; a program needn't handle non-finite values.
Results may differ from a plain program's by a relative error of at most 0.03.
Values may be sent and summed in bfloat16 or wider, within the bound.
No kernel may reach another device: no remote copies, remote signals or barrier semaphores. Data moves between devices by JAX's collectives and lax.ppermute only.
A program may use at most 64 MiB of HBM per device.

v0:
```python
import jax
import jax.numpy as jnp
from jax import lax
from jax.sharding import PartitionSpec as P

step_size = 0.1


def from_behind(value, axis, steps):
    count = lax.axis_size(axis)
    leading, last = (max(0, -steps), min(count, count - steps))
    return lax.ppermute(value, axis, [(source, source + steps) for source in range(leading, last)])


def shortened(array):
    return jax.tree.map(lambda a: a.astype(jnp.bfloat16) if a.dtype == jnp.float32 else a, array)


def slope_of(inputs, weight_block):
    tangent = jnp.tanh(jnp.dot(inputs, weight_block, preferred_element_type=jnp.float32))
    return 1.0 - tangent * tangent


def back_product(scaled_rows, weight_block):
    return lax.dot_general(
        scaled_rows, weight_block, (((1,), (1,)), ((), ())), preferred_element_type=jnp.float32
    )


def body(states, weights, guess_points, cotangent):
    slab_count = lax.axis_size("layer")
    slab_index = lax.axis_index("layer")
    half_index = lax.axis_index("mp")
    layer_count, row_count, model_width = states.shape
    point_count = guess_points.shape[0]
    factor = layer_count // point_count
    columns = weights.shape[2]
    half_rows = row_count // lax.axis_size("mp")
    row_start = half_index * half_rows
    col_start = half_index * columns
    gathered = lax.all_gather(weights, "dp", axis=1, tiled=True)
    next_point = from_behind(guess_points[0], "layer", -1)
    terminal = jnp.where(
        slab_index == slab_count - 1, cotangent.astype(jnp.float32), next_point.astype(jnp.float32)
    )
    guess_wide = guess_points.astype(jnp.float32)
    slopes = [slope_of(states[layer_id], gathered[layer_id]) for layer_id in range(layer_count)]

    def scale_columns(upper_adj, layer_id):
        own_part = lax.dynamic_slice_in_dim(upper_adj, col_start, columns, 1)
        return (own_part * slopes[layer_id]).astype(jnp.bfloat16)

    def fine_step(upper_adj, scaled_rows, layer_id):
        summed = lax.psum(back_product(scaled_rows, gathered[layer_id]), "mp")
        return upper_adj + step_size * summed

    upper_adj = terminal
    residuals = [None] * point_count
    for layer_id in range(layer_count - 1, -1, -1):
        relaxed = fine_step(upper_adj, scale_columns(upper_adj, layer_id), layer_id)
        if layer_id % factor == 0:
            residuals[layer_id // factor] = relaxed - guess_wide[layer_id // factor]
            upper_adj = guess_wide[layer_id // factor]
        else:
            upper_adj = relaxed
    residual_half = lax.dynamic_slice_in_dim(jnp.stack(residuals), row_start, half_rows, 1)
    coarse_weights = lax.all_gather(gathered[::factor], "mp", axis=2, tiled=True)
    state_half = lax.dynamic_slice_in_dim(states[::factor], row_start, half_rows, 1)
    coarse_slopes = jnp.stack([slope_of(state_half[0], coarse_weights[0])])

    def coarse_solve(incoming):
        carried = incoming.astype(jnp.float32)
        results = [None] * point_count
        scaled_rows = (carried * coarse_slopes[0]).astype(jnp.bfloat16)
        stepped = (
            carried
            + factor * step_size * back_product(scaled_rows, coarse_weights[0])
            + residual_half[0]
        )
        results[0] = stepped.astype(jnp.bfloat16)
        return jnp.stack(results)

    def solve_pair(operand_pair):
        return coarse_solve(operand_pair[0])

    def keep_pair(operand_pair):
        return operand_pair[1]

    def one_turn(turn_id, loop_state):
        incoming, errors = loop_state
        errors = lax.cond(
            turn_id == slab_count - 1 - slab_index, solve_pair, keep_pair, (incoming, errors)
        )
        incoming = from_behind(shortened(errors[0]), "layer", -1)
        return (incoming, errors)

    start_in = jnp.zeros((half_rows, model_width), jnp.bfloat16)
    start_errors = jnp.zeros((point_count, half_rows, model_width), jnp.bfloat16)
    incoming, errors = lax.fori_loop(0, slab_count - 1, one_turn, (start_in, start_errors))
    errors = lax.cond(slab_index == 0, solve_pair, keep_pair, (incoming, errors))
    adjoint_parts = [None] * layer_count
    scaled_parts = [None] * layer_count
    spread = lax.all_gather(
        shortened(jnp.concatenate([errors, incoming[None]], 0)), "mp", axis=1, tiled=True
    )
    upper_adj = terminal + spread[point_count].astype(jnp.float32)
    for layer_id in range(layer_count - 1, -1, -1):
        scaled_rows = scale_columns(upper_adj, layer_id)
        if layer_id % factor == 0:
            current = guess_wide[layer_id // factor] + spread[layer_id // factor].astype(
                jnp.float32
            )
        else:
            current = fine_step(upper_adj, scaled_rows, layer_id)
        adjoint_parts[layer_id] = lax.dynamic_slice_in_dim(current, col_start, columns, 1).astype(
            jnp.bfloat16
        )
        scaled_parts[layer_id] = scaled_rows
        upper_adj = current
    adjoint_out = jnp.stack(adjoint_parts)
    scaled_out = jnp.stack(scaled_parts)
    partial_terms = jnp.einsum(
        "lrd,lrh->ldh", states, scaled_out, preferred_element_type=jnp.float32
    )
    weight_grads = step_size * lax.psum_scatter(
        partial_terms.astype(jnp.bfloat16), "dp", scatter_dimension=1, tiled=True
    ).astype(jnp.float32)
    return (adjoint_out, weight_grads)


def solution(mesh):
    return jax.shard_map(
        body,
        mesh=mesh,
        in_specs=(
            P("layer", "dp", None),
            P("layer", "dp", "mp"),
            P("layer", "dp", None),
            P("dp", None),
        ),
        out_specs=(P("layer", "dp", "mp"), P("layer", "dp", "mp")),
        check_vma=False,
    )
```

profile of v0, /device:TPU:1, one launch (start us, length us, event | category | flops | bytes accessed | tf_op | source)
XLA Modules:
  0.0 934.7 jit_solution(8836864910243469288)
XLA Ops:
  8.0 8.7 collective-permute-start.1
  19.1 53.4 %all-gather.3.cloned.1.call-done = bf16[4,1024,512]{2,1,0:T(8,128)(2,1)} async-done(((bf16[4,128,512]{2,1,0:T(8,128)(2,1)}), bf16[4,1024,512]{2,1,0:T(8,128)(2,1)}) %all-gather.3.cloned.1.call-update) | async-done | bytes 4194320 | tf_op jit(solution)/shard_map/all_gather | solution.py:41
  78.4 59.1 %all-reduce.8.cloned.1.call-done = f32[128,1024]{1,0:T(8,128)} async-done(((f32[128,1024]{1,0:T(8,128)}), f32[128,1024]{1,0:T(8,128)}) %all-reduce.8.cloned.1.call-update) | async-done | bytes 524304 | tf_op jit(solution)/shard_map/psum | solution.py:54
  142.7 56.4 %all-reduce.10.cloned.1.call-done = f32[128,1024]{1,0:T(8,128)} async-done(((f32[128,1024]{1,0:T(8,128)}), f32[128,1024]{1,0:T(8,128)}) %all-reduce.10.cloned.1.call-update) | async-done | bytes 524304 | tf_op jit(solution)/shard_map/psum | solution.py:54
  207.4 53.4 %all-reduce.12.cloned.1.call-done = f32[128,1024]{1,0:T(8,128)} async-done(((f32[128,1024]{1,0:T(8,128)}), f32[128,1024]{1,0:T(8,128)}) %all-reduce.12.cloned.1.call-update) | async-done | bytes 524304 | tf_op jit(solution)/shard_map/psum | solution.py:54
  265.6 62.4 %all-gather.5.cloned.1.call-done = bf16[1,1024,1024]{2,1,0:T(8,128)(2,1)} async-done(((bf16[1,1024,512]{2,1,0:T(8,128)(2,1)}), bf16[1,1024,1024]{2,1,0:T(8,128)(2,1)}) %all-gather.5.cloned.1.call-update) | async-done | bytes 2097168 | tf_op jit(solution)/shard_map/all_gather | solution.py:67
  330.0 59.3 %all-reduce.14.cloned.1.call-done = f32[128,1024]{1,0:T(8,128)} async-done(((f32[128,1024]{1,0:T(8,128)}), f32[128,1024]{1,0:T(8,128)}) %all-reduce.14.cloned.1.call-update) | async-done | bytes 524304 | tf_op jit(solution)/shard_map/psum | solution.py:54
  390.3 250.6 %while.23 = (s32[]{:T(128)}, bf16[64,1024]{1,0:T(8,128)(2,1)S(1)}, bf16[1,64,1024]{2,1,0:T(8,128)(2,1)S(1)}, s32[]{:T(128)}, f32[64,1024]{1,0:T(8,128)S(1)}, /*i...) while((s32[]{:T(128)}, bf16[64,1024]{1,0:T(8,128)(2,1)S(1)}, ...), condition=%wide.region_7.8_spmd, body=%wide.region_4.7_spmd.sunk | while | flops 134742016 | bytes 3408051 | solution.py:99
  477.4 6.5 collective-permute-done
  494.2 6.5 collective-permute-done
  502.6 6.5 collective-permute-done
  519.4 6.5 collective-permute-done
  536.1 6.5 collective-permute-done
  552.9 6.5 collective-permute-done
  569.7 6.5 collective-permute-done
  586.5 6.5 collective-permute-done
  603.2 6.5 collective-permute-done
  611.6 20.7 %collective-permute-done = bf16[64,1024]{1,0:T(8,128)(2,1)S(1)} collective-permute-done((bf16[64,1024]{1,0:T(8,128)(2,1)S(1)}, bf16[64,1024]{1,0:T(8,128)(2,1)S(1)}, u32[]{:S(2)}, u32[]{:S(2)}) %collective-permute-start) | collective-permute-done | bytes 131104 | tf_op jit(solution)/shard_map/while/body/eval_jaxpr/ppermute | solution.py:12
  641.0 15.2 %all_gather.11 = bf16[2,128,1024]{2,1,0:T(8,128)(2,1)S(1)} all-gather(bf16[2,64,1024]{2,1,0:T(8,128)(2,1)S(1)} %pad_maximum_fusion.1), channel_id=1, replica_groups=mesh['layer'=32,'dp'=8,'mp'=2] {'mp'}, dimensions={1}, use_global_device_ids=true | all-gather | bytes 786432 | tf_op jit(solution)/shard_map/all_gather | solution.py:103
  658.9 69.1 %all-reduce.16.cloned.1.call-done = f32[128,1024]{1,0:T(8,128)} async-done(((f32[128,1024]{1,0:T(8,128)}), f32[128,1024]{1,0:T(8,128)}) %all-reduce.16.cloned.1.call-update) | async-done | bytes 524304 | tf_op jit(solution)/shard_map/psum | solution.py:54
  731.7 58.0 %all-reduce.18.cloned.1.call-done = f32[128,1024]{1,0:T(8,128)} async-done(((f32[128,1024]{1,0:T(8,128)}), f32[128,1024]{1,0:T(8,128)}) %all-reduce.18.cloned.1.call-update) | async-done | bytes 524304 | tf_op jit(solution)/shard_map/psum | solution.py:54
  793.4 58.0 %all-reduce.20.cloned.1.call-done = f32[128,1024]{1,0:T(8,128)} async-done(((f32[128,1024]{1,0:T(8,128)}), f32[128,1024]{1,0:T(8,128)}) %all-reduce.20.cloned.1.call-update) | async-done | bytes 524304 | tf_op jit(solution)/shard_map/psum | solution.py:54
  856.9 7.8 copy.11
  871.3 53.3 %reduce-scatter.4.cloned.1.call-done = bf16[128,2048]{1,0:T(8,128)(2,1)} async-done(((bf16[1024,2048]{1,0:T(8,128)(2,1)}), bf16[128,2048]{1,0:T(8,128)(2,1)}) %reduce-scatter.4.cloned.1.call-update) | async-done | bytes 524304
  (156 shorter events, 229.3 us)
Async XLA Ops:
  7.2 65.3 %all-gather.3.cloned.1.call-start = ((), (), s32[]{:S(2)}) async-start(), calls=%async_computation.1 | async-start | bytes 4718592 | tf_op jit(solution)/shard_map/all_gather | solution.py:41
  7.9 129.6 %all-reduce.8.cloned.1.call-start = ((), (), s32[]{:S(2)}) async-start(), calls=%async_computation.3 | async-start | bytes 1048576 | tf_op jit(solution)/shard_map/psum | solution.py:54
  8.0 10.1 %collective-permute-start.1 = (bf16[128,1024]{1,0:T(8,128)(2,1)}, bf16[128,1024]{1,0:T(8,128)(2,1)S(1)}, u32[]{:S(2)}, u32[]{:S(2)}) collective-permute-start(bf16[128,1024]{1,0:T(8,128)(2,1)} %bitcast.126), channel_id=1, source_target_pairs={{16,0},{32,16},{48,32},{64,48},{80,64},{96,80},{112,96},{128,112},... | collective-permute-start | bytes 786440 | tf_op jit(solution)/shard_map/ppermute | solution.py:12
  76.8 122.4 %all-reduce.10.cloned.1.call-start = ((), (), s32[]{:S(2)}) async-start(), calls=%async_computation.4 | async-start | bytes 1048576 | tf_op jit(solution)/shard_map/psum | solution.py:54
  141.1 119.7 %all-reduce.12.cloned.1.call-start = ((), (), s32[]{:S(2)}) async-start(), calls=%async_computation.5 | async-start | bytes 1048576 | tf_op jit(solution)/shard_map/psum | solution.py:54
  202.8 125.2 %all-gather.5.cloned.1.call-start = ((), (), s32[]{:S(2)}) async-start(), calls=%async_computation.2 | async-start | bytes 3145728 | tf_op jit(solution)/shard_map/all_gather | solution.py:67
  205.1 184.2 %all-reduce.14.cloned.1.call-start = ((), (), s32[]{:S(2)}) async-start(), calls=%async_computation.6 | async-start | bytes 1048576 | tf_op jit(solution)/shard_map/psum | solution.py:54
  264.5 463.5 %all-reduce.16.cloned.1.call-start = ((), (), s32[]{:S(2)}) async-start(), calls=%async_computation.7 | async-start | bytes 1048576 | tf_op jit(solution)/shard_map/psum | solution.py:54
  467.1 8.4 collective-permute-start
  475.5 8.4 collective-permute-start
  483.9 8.4 collective-permute-start
  492.3 8.4 collective-permute-start
  500.7 8.4 collective-permute-start
  509.1 8.4 collective-permute-start
  517.4 8.4 collective-permute-start
  534.2 8.4 collective-permute-start
  551.0 8.4 collective-permute-start
  567.8 8.4 collective-permute-start
  584.5 8.4 collective-permute-start
  601.3 8.4 collective-permute-start
  609.7 22.6 %collective-permute-start = (bf16[64,1024]{1,0:T(8,128)(2,1)S(1)}, bf16[64,1024]{1,0:T(8,128)(2,1)S(1)}, u32[]{:S(2)}, u32[]{:S(2)}) collective-permute-start(bf16[64,1024]{1,0:T(8,128)(2,1)S(1)} %bitcast.125), channel_id=1, source_target_pairs={{16,0},{32,16},{48,32},{64,48},{80,64},{96,80},{112,96},{128,112},... | collective-permute-start | bytes 393224 | tf_op jit(solution)/shard_map/while/body/eval_jaxpr/ppermute | solution.py:12
  658.9 130.8 %all-reduce.18.cloned.1.call-start = ((), (), s32[]{:S(2)}) async-start(), calls=%async_computation.8 | async-start | bytes 1048576 | tf_op jit(solution)/shard_map/psum | solution.py:54
  731.7 119.7 %all-reduce.20.cloned.1.call-start = ((), (), s32[]{:S(2)}) async-start(), calls=%async_computation.9 | async-start | bytes 1048576 | tf_op jit(solution)/shard_map/psum | solution.py:54
  793.4 131.2 %reduce-scatter.4.cloned.1.call-start = ((), (), s32[]{:S(2)}) async-start(), calls=%async_computation.10 | async-start | bytes 4718592
  (23 other events, 529.6 us)
Sparse Core Ops, SparseCore 0:
  10.1 62.3 all-gather.2
  76.9 60.5 all-reduce.7
  141.2 57.8 all-reduce.9
  202.9 57.8 all-reduce.11
  263.3 64.5 all-gather.4
  331.3 57.9 all-reduce.13
  659.0 68.9 all-reduce.15
  731.8 57.8 all-reduce.17
  793.5 57.8 all-reduce.19
  870.4 54.0 reduce-scatter.3
where the time goes:
time: 937 us; the launch traced here: 935 us
  waiting for transfers between devices  772 us (82%)
  starting transfers between devices  69.2 us (7%)
  matrix products  33.6 us (4%)
  local copies, waits for them, and re-layouts  18.9 us (2%)
  blocking collectives  15.2 us (2%)
  between operations  14.4 us (2%)
  other arithmetic  10.7 us (1%)
    psum x7, waiting for transfers between devices, fine_step(): summed = lax.psum(back_product(scaled_rows, gathered[layer_id]), 'mp')  413 us
    ppermute x32, waiting for transfers between devices, from_behind(): lax.ppermute(value, axis, [(source, source + steps) for source in range(l...  189 us
    ppermute x32, starting transfers between devices, from_behind(): lax.ppermute(value, axis, [(source, source + steps) for source in range(l...  68.8 us
    all_gather x1, waiting for transfers between devices, body(): lax.all_gather(gathered[::factor], 'mp', axis=2, tiled=True)  62.4 us
    unnamed x11, waiting for transfers between devices  54.1 us
    all_gather x1, waiting for transfers between devices, body(): gathered = lax.all_gather(weights, 'dp', axis=1, tiled=True)  53.4 us
    dot_general x8, matrix products, back_product(): lax.dot_general(scaled_rows, weight_block, (((1,), (1,)), ((), ())), pref...  20 us
  transfers between devices with their start and end apart: 42, of which 42 were waited for; matrix products, arithmetic and copies ran while one was open for 2% of the time, Pallas kernels for 0%

commit v1 on v0

--- a/solution.py
+++ b/solution.py
@@ -38,7 +38,9 @@
     half_rows = row_count // lax.axis_size("mp")
     row_start = half_index * half_rows
     col_start = half_index * columns
-    gathered = lax.all_gather(weights, "dp", axis=1, tiled=True)
+    gathered = jnp.concatenate(
+        lax.all_to_all(jnp.stack([weights] * lax.axis_size("dp")), "dp", 0, 0), axis=1
+    )
     next_point = from_behind(guess_points[0], "layer", -1)
     terminal = jnp.where(
         slab_index == slab_count - 1, cotangent.astype(jnp.float32), next_point.astype(jnp.float32)

time: 937 us -> 989 us (1.055)
  waiting for transfers between devices: 772 us -> 816 us
  matrix products: 33.6 us -> 22.5 us
  local copies, waits for them, and re-layouts: 18.9 us -> 29.7 us
    all_to_all x0 -> x1, waiting for transfers between devices: none -> 83.8 us  [body(): lax.all_to_all(jnp.stack([weights] * lax.axis_size('dp')), 'dp', 0, 0)]
    all_gather x1 -> x0, waiting for transfers between devices: 53.4 us -> none  [body(): gathered = lax.all_gather(weights, 'dp', axis=1, tiled=True)]
    unnamed x14 -> x64, local copies, waits for them, and re-layouts: 16.6 us -> 21.8 us
    unnamed x11 -> x10, waiting for transfers between devices: 54.1 us -> 52.8 us
  transfers between devices with their start and end apart: 42 -> 42, of which waited for: 42 -> 42; matrix products, arithmetic and copies ran while one was open for 2% -> 1% of each run, Pallas kernels for 0% -> 0%
where the time goes in v1:
time: 989 us; the launch traced here: 987 us
  waiting for transfers between devices  816 us (83%)
  starting transfers between devices  73.8 us (7%)
  local copies, waits for them, and re-layouts  29.7 us (3%)
  matrix products  22.5 us (2%)
  blocking collectives  15.3 us (2%)
  other arithmetic  14.4 us (1%)
  between operations  14.2 us (1%)
    psum x7, waiting for transfers between devices, fine_step(): summed = lax.psum(back_product(scaled_rows, gathered[layer_id]), 'mp')  420 us
    ppermute x32, waiting for transfers between devices, from_behind(): lax.ppermute(value, axis, [(source, source + steps) for source in range(l...  197 us
    all_to_all x1, waiting for transfers between devices, body(): lax.all_to_all(jnp.stack([weights] * lax.axis_size('dp')), 'dp', 0, 0)  83.8 us
    ppermute x32, starting transfers between devices, from_behind(): lax.ppermute(value, axis, [(source, source + steps) for source in range(l...  65.7 us
    all_gather x1, waiting for transfers between devices, body(): lax.all_gather(gathered[::factor], 'mp', axis=2, tiled=True)  62.5 us
    unnamed x10, waiting for transfers between devices  52.8 us
    unnamed x64, local copies, waits for them, and re-layouts  21.8 us
  transfers between devices with their start and end apart: 42, of which 42 were waited for; matrix products, arithmetic and copies ran while one was open for 1% of the time, Pallas kernels for 0%

profile of v1, /device:TPU:1, one launch (start us, length us, event | category | flops | bytes accessed | tf_op | source)
XLA Modules:
  0.0 986.8 jit_solution(5481136650381966621)
XLA Ops:
  10.7 7.8 all-to-all-start
  27.8 83.8 %all-to-all-done = bf16[8,4,128,512]{3,2,1,0:T(8,128)(2,1)} async-done(((bf16[8,4,128,512]{3,2,1,0:T(8,128)(2,1)}), bf16[8,4,128,512]{3,2,1,0:T(8,128)(2,1)}, u32[]{:S(2)}, u32[]{:S(2)}) %all-to-all-start) | async-done | bytes 4194336 | tf_op jit(solution)/shard_map/all_to_all | solution.py:42
  119.3 63.1 %all-reduce.8.cloned.1.call-done = f32[128,1024]{1,0:T(8,128)} async-done(((f32[128,1024]{1,0:T(8,128)}), f32[128,1024]{1,0:T(8,128)}) %all-reduce.8.cloned.1.call-update) | async-done | bytes 524304 | tf_op jit(solution)/shard_map/psum | solution.py:56
  186.2 57.6 %all-reduce.10.cloned.1.call-done = f32[128,1024]{1,0:T(8,128)} async-done(((f32[128,1024]{1,0:T(8,128)}), f32[128,1024]{1,0:T(8,128)}) %all-reduce.10.cloned.1.call-update) | async-done | bytes 524304 | tf_op jit(solution)/shard_map/psum | solution.py:56
  248.6 56.4 %all-reduce.12.cloned.1.call-done = f32[128,1024]{1,0:T(8,128)} async-done(((f32[128,1024]{1,0:T(8,128)}), f32[128,1024]{1,0:T(8,128)}) %all-reduce.12.cloned.1.call-update) | async-done | bytes 524304 | tf_op jit(solution)/shard_map/psum | solution.py:56
  309.8 62.5 %all-gather.2.cloned.1.call-done = bf16[1,1024,1024]{2,1,0:T(8,128)(2,1)} async-done(((bf16[1,1024,512]{2,1,0:T(8,128)(2,1)}), bf16[1,1024,1024]{2,1,0:T(8,128)(2,1)}) %all-gather.2.cloned.1.call-update) | async-done | bytes 2097168 | tf_op jit(solution)/shard_map/all_gather | solution.py:69
  375.2 57.8 %all-reduce.14.cloned.1.call-done = f32[128,1024]{1,0:T(8,128)} async-done(((f32[128,1024]{1,0:T(8,128)}), f32[128,1024]{1,0:T(8,128)}) %all-reduce.14.cloned.1.call-update) | async-done | bytes 524304 | tf_op jit(solution)/shard_map/psum | solution.py:56
  434.8 257.1 %while.23 = (s32[]{:T(128)}, bf16[64,1024]{1,0:T(8,128)(2,1)S(1)}, bf16[1,64,1024]{2,1,0:T(8,128)(2,1)}, s32[]{:T(128)}, f32[64,1024]{1,0:T(8,128)}, /*index=5*/...) while((s32[]{:T(128)}, bf16[64,1024]{1,0:T(8,128)(2,1)S(1)}, ...), condition=%wide.region_7.8_spmd, body=%wide.region_4.7_spmd.sunk | while | flops 134742016 | bytes 3408051 | solution.py:101
  516.0 6.7 collective-permute-done
  524.6 6.7 collective-permute-done
  541.8 6.7 collective-permute-done
  550.4 6.7 collective-permute-done
  559.0 6.7 collective-permute-done
  567.6 6.7 collective-permute-done
  584.8 6.7 collective-permute-done
  593.4 6.7 collective-permute-done
  602.0 6.7 collective-permute-done
  662.2 20.9 %collective-permute-done = bf16[64,1024]{1,0:T(8,128)(2,1)S(1)} collective-permute-done((bf16[64,1024]{1,0:T(8,128)(2,1)}, bf16[64,1024]{1,0:T(8,128)(2,1)S(1)}, u32[]{:S(2)}, u32[]{:S(2)}) %collective-permute-start) | collective-permute-done | bytes 131104 | tf_op jit(solution)/shard_map/while/body/eval_jaxpr/ppermute | solution.py:12
  693.0 15.3 %all_gather.7 = bf16[2,128,1024]{2,1,0:T(8,128)(2,1)S(1)} all-gather(bf16[2,64,1024]{2,1,0:T(8,128)(2,1)S(1)} %pad_maximum_fusion.1), channel_id=1, replica_groups=mesh['layer'=32,'dp'=8,'mp'=2] {'mp'}, dimensions={1}, use_global_device_ids=true | all-gather | bytes 786432 | tf_op jit(solution)/shard_map/all_gather | solution.py:105
  711.8 69.2 %all-reduce.16.cloned.1.call-done = f32[128,1024]{1,0:T(8,128)} async-done(((f32[128,1024]{1,0:T(8,128)}), f32[128,1024]{1,0:T(8,128)}) %all-reduce.16.cloned.1.call-update) | async-done | bytes 524304 | tf_op jit(solution)/shard_map/psum | solution.py:56
  784.7 58.0 %all-reduce.18.cloned.1.call-done = f32[128,1024]{1,0:T(8,128)} async-done(((f32[128,1024]{1,0:T(8,128)}), f32[128,1024]{1,0:T(8,128)}) %all-reduce.18.cloned.1.call-update) | async-done | bytes 524304 | tf_op jit(solution)/shard_map/psum | solution.py:56
  845.9 58.2 %all-reduce.20.cloned.1.call-done = f32[128,1024]{1,0:T(8,128)} async-done(((f32[128,1024]{1,0:T(8,128)}), f32[128,1024]{1,0:T(8,128)}) %all-reduce.20.cloned.1.call-update) | async-done | bytes 524304 | tf_op jit(solution)/shard_map/psum | solution.py:56
  909.3 7.9 copy.11
  924.9 52.1 %reduce-scatter.4.cloned.1.call-done = bf16[128,2048]{1,0:T(8,128)(2,1)} async-done(((bf16[1024,2048]{1,0:T(8,128)(2,1)}), bf16[128,2048]{1,0:T(8,128)(2,1)}) %reduce-scatter.4.cloned.1.call-update) | async-done | bytes 524304
  (206 shorter events, 243.9 us)
Async XLA Ops:
  10.7 100.9 %all-to-all-start = ((bf16[8,4,128,512]{3,2,1,0:T(8,128)(2,1)}), bf16[8,4,128,512]{3,2,1,0:T(8,128)(2,1)}, u32[]{:S(2)}, u32[]{:S(2)}) async-start(bf16[8,4,128,512]{3,2,1,0:T(8,128)(2,1)} %stack.48), calls=%async_computation | async-start | bytes 8388608 | tf_op jit(solution)/shard_map/all_to_all | solution.py:42
  18.5 163.9 %all-reduce.8.cloned.1.call-start = ((), (), s32[]{:S(2)}) async-start(), calls=%async_computation.3 | async-start | bytes 1048576 | tf_op jit(solution)/shard_map/psum | solution.py:56
  117.9 125.9 %all-reduce.10.cloned.1.call-start = ((), (), s32[]{:S(2)}) async-start(), calls=%async_computation.4 | async-start | bytes 1048576 | tf_op jit(solution)/shard_map/psum | solution.py:56
  185.8 119.3 %all-reduce.12.cloned.1.call-start = ((), (), s32[]{:S(2)}) async-start(), calls=%async_computation.5 | async-start | bytes 1048576 | tf_op jit(solution)/shard_map/psum | solution.py:56
  247.0 125.3 %all-gather.2.cloned.1.call-start = ((), (), s32[]{:S(2)}) async-start(), calls=%async_computation.2 | async-start | bytes 3145728 | tf_op jit(solution)/shard_map/all_gather | solution.py:69
  247.6 185.4 %all-reduce.14.cloned.1.call-start = ((), (), s32[]{:S(2)}) async-start(), calls=%async_computation.6 | async-start | bytes 1048576 | tf_op jit(solution)/shard_map/psum | solution.py:56
  308.8 472.2 %all-reduce.16.cloned.1.call-start = ((), (), s32[]{:S(2)}) async-start(), calls=%async_computation.7 | async-start | bytes 1048576 | tf_op jit(solution)/shard_map/psum | solution.py:56
  514.1 8.6 collective-permute-start
  522.7 8.6 collective-permute-start
  539.9 8.6 collective-permute-start
  548.5 8.6 collective-permute-start
  557.1 8.6 collective-permute-start
  565.7 8.6 collective-permute-start
  582.9 8.6 collective-permute-start
  591.5 8.6 collective-permute-start
  600.1 8.6 collective-permute-start
  608.7 8.6 collective-permute-start
  625.9 8.6 collective-permute-start
  634.5 8.6 collective-permute-start
  643.1 8.6 collective-permute-start
  660.3 22.8 %collective-permute-start = (bf16[64,1024]{1,0:T(8,128)(2,1)}, bf16[64,1024]{1,0:T(8,128)(2,1)S(1)}, u32[]{:S(2)}, u32[]{:S(2)}) collective-permute-start(bf16[64,1024]{1,0:T(8,128)(2,1)} %bitcast.134), channel_id=1, source_target_pairs={{16,0},{32,16},{48,32},{64,48},{80,64},{96,80},{112,96},{128,112},... | collective-permute-start | bytes 393224 | tf_op jit(solution)/shard_map/while/body/eval_jaxpr/ppermute | solution.py:12
  711.8 130.9 %all-reduce.18.cloned.1.call-start = ((), (), s32[]{:S(2)}) async-start(), calls=%async_computation.8 | async-start | bytes 1048576 | tf_op jit(solution)/shard_map/psum | solution.py:56
  784.7 119.4 %all-reduce.20.cloned.1.call-start = ((), (), s32[]{:S(2)}) async-start(), calls=%async_computation.9 | async-start | bytes 1048576 | tf_op jit(solution)/shard_map/psum | solution.py:56
  845.8 131.2 %reduce-scatter.4.cloned.1.call-start = ((), (), s32[]{:S(2)}) async-start(), calls=%async_computation.10 | async-start | bytes 4718592
  (48 other events, 980.5 us)
Sparse Core Ops, SparseCore 0:
  118.0 64.3 all-reduce.7
  185.9 57.8 all-reduce.9
  247.1 57.9 all-reduce.11
  307.6 64.5 all-gather.1
  375.0 57.9 all-reduce.13
  711.9 69.1 all-reduce.15
  784.8 57.8 all-reduce.17
  846.1 57.8 all-reduce.19
  922.9 54.0 reduce-scatter.3
